TPU v7x, 256 devices: a whole 4x4x8 slice. The times are simulated.
256 devices in a mesh: slab: 16 (over z_hi, x, core), chan: 16 (over y, z_lo).
Axes of the slice: x: 4, y: 4, z: 8 (z_hi: 2, z_lo: 4; z = z_hi * 4 + z_lo), core: 2. Of those that a mesh axis runs over, the one named last changes fastest.
Arguments:
- activations: bfloat16 [2, 128, 32, 16384], P(None, 'chan', 'slab'), may hold values from -6 to 6
- out_grad: bfloat16 [2, 256, 16, 4096], P(None, 'chan', 'slab'), may hold values from -6 to 6
- weights: bfloat16 [27, 128, 256], P(None, 'chan'), may hold values from -0.109375 to 0.109375
Outputs:
- input_grad: bfloat16 [2, 128, 32, 16384], P(None, 'chan', 'slab')
- weight_grad: float32 [27, 128, 256], P(None, 'chan', 'slab')
All inputs are finite; a program needn't handle non-finite values.
Results may differ from a plain program's by a relative error of at most 0.001.
Values may be sent and summed in bfloat16 or wider, within the bound.
A program may use at most 128 MiB of HBM per device.

v0:
```python
import math
import jax
import jax.numpy as jnp
from jax import lax
from jax.sharding import PartitionSpec as P

EDGE = 128


def from_behind(x, axis, by):
    count = lax.axis_size(axis)
    pairs = [(i, i + by) for i in range(count) if 0 <= i + by < count]
    return lax.ppermute(x, axis, pairs)


def flat_back(values, amount):
    zero_part = jnp.zeros(values.shape[:-1] + (amount,), values.dtype)
    return jnp.concatenate([zero_part, values[..., : values.shape[-1] - amount]], axis=-1)


def flat_ahead(values, amount):
    zero_part = jnp.zeros(values.shape[:-1] + (amount,), values.dtype)
    return jnp.concatenate([values[..., amount:], zero_part], axis=-1)


def column_index(length, half_edge):
    return lax.iota(jnp.int32, length) % half_edge


def tap_view(volume, row_tap, col_tap, half_edge):
    cells = half_edge * half_edge
    row_phase = 0 if row_tap == 1 else 1
    col_phase = 0 if col_tap == 1 else 1
    block = row_phase * 2 + col_phase
    picked = volume[..., block * cells : (block + 1) * cells]
    if row_tap == 0:
        picked = flat_back(picked, half_edge)
    if col_tap == 0:
        picked = flat_back(picked, 1)
        keep_mask = column_index(cells, half_edge) != 0
        picked = jnp.where(keep_mask, picked, jnp.zeros_like(picked))
    return picked


def assemble(fetch, half_edge, block_cells):
    last_column = column_index(block_cells, half_edge) == half_edge - 1
    rows_even = [fetch(1, col_tap) for col_tap in range(3)]
    rows_odd = [
        fetch(2, col_tap) + flat_ahead(fetch(0, col_tap), half_edge) for col_tap in range(3)
    ]
    phases = []
    for rows in (rows_even, rows_odd):
        phases.append(rows[1])
        moved = flat_ahead(rows[0], 1)
        phases.append(rows[2] + jnp.where(last_column, jnp.zeros_like(moved), moved))
    return jnp.concatenate(phases, axis=-1)


def body(activations, out_grad, weights):
    samples, chan_local, planes, plane_cells = activations.shape
    half_edge = EDGE // 2
    cells = half_edge * half_edge
    out_planes = planes // 2
    phased = activations.reshape(samples, chan_local, out_planes, 2, plane_cells)
    even_planes = phased[:, :, :, 0]
    odd_planes = phased[:, :, :, 1]
    previous = from_behind(odd_planes[:, :, out_planes - 1], "slab", 1)
    odd_before = jnp.concatenate([previous[:, :, None], odd_planes[:, :, : out_planes - 1]], axis=2)
    depth_views = (odd_before, even_planes, odd_planes)
    following = from_behind(out_grad[:, :, 0], "slab", -1)
    source = jnp.concatenate([out_grad, following[:, :, None]], axis=2)
    signal = lax.all_gather(source, "chan", axis=1, tiled=True)
    own_planes = signal[:, :, :out_planes]
    pieces = []
    for depth_tap in range(3):
        stacked = jnp.stack(
            [
                tap_view(depth_views[depth_tap], row_tap, col_tap, half_edge)
                for row_tap in range(3)
                for col_tap in range(3)
            ]
        )
        pieces.append(
            jnp.einsum("tbcdp,bkdp->tck", stacked, own_planes, preferred_element_type=jnp.float32)
        )
    local_grad = jnp.concatenate(pieces, axis=0)
    total_cells = samples * out_planes * lax.axis_size("slab") * half_edge * half_edge
    weight_grad = lax.psum_scatter(local_grad, "slab", scatter_dimension=2, tiled=True) * (
        1.0 / math.sqrt(total_cells)
    )
    first_block = signal[:, :, 1:]
    blocks = (first_block, own_planes, own_planes)
    folded = []
    for depth_tap in range(3):
        groups = jnp.einsum(
            "tck,bkdp->tbcdp",
            weights[9 * depth_tap : 9 * depth_tap + 9],
            blocks[depth_tap],
            preferred_element_type=jnp.float32,
        )

        def fetch(row_tap, col_tap, groups=groups):
            return groups[3 * row_tap + col_tap]

        folded.append(assemble(fetch, half_edge, cells))
    shifted = folded[0]
    odd_out = folded[2] + shifted
    chan_rows = folded[1].shape[1]
    kept_cells = 4 * cells
    local_grad_in = (
        jnp.stack([folded[1], odd_out], axis=3)
        .reshape(samples, chan_rows, planes, kept_cells)
        .astype(jnp.bfloat16)
    )
    return (local_grad_in, weight_grad)


def solution(mesh):
    placed = (P(None, "chan", "slab", None), P(None, "chan", "slab", None), P(None, "chan", None))
    return jax.shard_map(
        body,
        mesh=mesh,
        in_specs=placed,
        out_specs=(P(None, "chan", "slab", None), P(None, "chan", "slab")),
        check_vma=False,
    )
```

profile of v0, /device:TPU:8, one launch (start us, length us, event | category | flops | bytes accessed | tf_op | source)
XLA Modules:
  0.0 308.4 jit_solution(10184188523158755231)
XLA Ops:
  7.2 1.3 collective-permute-start
  8.5 1.8 copy.115
  10.4 3.1 collective-permute-start.1
  14.3 0.8 bitcast_dynamic-update-slice_fusion.10
  15.1 0.9 bitcast_dynamic-update-slice_fusion.8
  16.1 0.8 bitcast_dynamic-update-slice_fusion.7
  16.8 0.8 pad_maximum_fusion.1
  17.8 0.7 bitcast_dynamic-update-slice_fusion.6
  18.5 0.7 fusion.56
  19.2 0.7 fusion.55
  19.9 0.8 bitcast_dynamic-update-slice_fusion.5
  20.6 0.7 fusion.58
  21.3 0.7 fusion.54
  21.9 0.7 fusion.53
  23.5 184.6 %all-gather.2.cloned.1.call-done = bf16[2,256,2,4096]{3,1,0,2:T(8,128)(2,1)} async-done(((bf16[2,16,2,4096]{3,1,0,2:T(8,128)(2,1)}), bf16[2,256,2,4096]{3,1,0,2:T(8,128)(2,1)}) %all-gather.2.cloned.1.call-update) | async-done | bytes 8388624 | tf_op jit(solution)/shard_map/all_gather | solution.py:72
  208.1 3.1 %convolution_bitcast_fusion = f32[9,2,8,1,4096]{4,0,2,1,3:T(8,128)S(1)} fusion(bf16[2,256,2,4096]{3,1,0,2:T(8,128)(2,1)} %all-gather.2.cloned.1.call-done, bf16[9,8,256]{2,1,0:T(8,128)(2,1)S(1)} %get-tuple-element.47), kind=kOutput, calls=%fused_computation | convolution fusion | flops 301989888 | bytes 6590464 | tf_op jit(solution)/shard_map/tck,bkdp->tbcdp/dot_general | solution.py:95
  211.5 1.0 fusion.72
  212.5 1.5 copy-done.6
  214.1 1.4 fusion.21
  215.5 1.4 fusion.16
  216.9 1.4 fusion.26
  218.3 1.4 copy.59
  219.8 3.0 convolution_bitcast_fusion.2
  224.1 0.6 slice.345
  225.9 3.0 convolution_bitcast_fusion.1
  230.8 1.4 pad_add_fusion.2
  232.1 3.2 %fusion.52 = (bf16[2,8,1,4096]{3,2,1,0:T(2,128)(2,1)S(1)}, bf16[2,8,1,4096]{3,2,1,0:T(2,128)(2,1)S(1)}) fusion(f32[9,2,8,1,4096]{4,0,2,1,3:T(8,128)} %copy-done, f32[2,8,1,4032]{3,2,1,0:T(1,128)S(1)} %slice.342, f32[2,8,1,4095]{3,2,1,0:T(1,128)S(1)} %pad_add_fusion.2, pred[4096]{0:T(1024)(128)(4,1)S(1)} %fusion.70, f32[2,8,1,4032]{3,2,1,0:T(1,128)S(1)} %slice.345), kind=kLoop, calls=%fused_computation.84 | loop fusion | flops 393216 | bytes 1568704 | tf_op jit(solution)/shard_map/convert.5
  235.4 1.1 pad_maximum_fusion
  237.3 2.1 copy.60
  239.4 60.7 %reduce-scatter.2.cloned.1.call-done = f32[27,8,16]{0,1,2:T(8,128)} async-done(((f32[27,8,256]{0,1,2:T(8,128)}), f32[27,8,16]{0,1,2:T(8,128)}) %reduce-scatter.2.cloned.1.call-update) | async-done | bytes 13840 | tf_op jit(solution)/shard_map/reduce_scatter | solution.py:88
  300.1 0.8 broadcast_multiply_fusion
  300.9 0.6 copy.61
  (73 shorter events, 7.0 us)
Async XLA Ops:
  7.2 200.9 %all-gather.2.cloned.1.call-start = ((), (), s32[]{:S(2)}) async-start(), calls=%async_computation.1 | async-start | bytes 8912896 | tf_op jit(solution)/shard_map/all_gather | solution.py:72
  7.2 9.6 %collective-permute-start = (bf16[2,16,4096]{2,1,0:T(8,128)(2,1)}, bf16[2,16,4096]{2,1,0:T(8,128)(2,1)S(1)}, u32[]{:S(2)}, u32[]{:S(2)}) collective-permute-start(bf16[2,16,4096]{2,1,0:T(8,128)(2,1)} %bitcast.307), channel_id=1, source_target_pairs={{16,0},{32,16},{48,32},{64,48},{80,64},{96,80},{112,96},{128,112},... | collective-permute-start | bytes 786440 | tf_op jit(solution)/shard_map/ppermute | solution.py:13
  10.4 12.3 %collective-permute-start.1 = (bf16[2,8,16384]{2,1,0:T(8,128)(2,1)S(1)}, bf16[2,8,16384]{2,1,0:T(8,128)(2,1)S(1)}, u32[]{:S(2)}, u32[]{:S(2)}) collective-permute-start(bf16[2,8,16384]{2,1,0:T(8,128)(2,1)S(1)} %get-tuple-element.32), channel_id=1, source_target_pairs={{0,16},{16,32},{32,48},{48,64},{64,80},{80,96},{96,112},{112,128},... | collective-permute-start | bytes 1572872 | tf_op jit(solution)/shard_map/ppermute | solution.py:13
  13.9 2.9 copy-start.1
  15.1 1.7 copy-start.3
  17.7 5.0 %copy-start.2 = (bf16[27,8,256]{2,1,0:T(8,128)(2,1)S(1)}, bf16[27,8,256]{2,1,0:T(8,128)(2,1)}, u32[]{:S(2)}) copy-start(bf16[27,8,256]{2,1,0:T(8,128)(2,1)} %param.5) | copy-start | bytes 331780
  17.7 282.4 %reduce-scatter.2.cloned.1.call-start = ((), (), s32[]{:S(2)}) async-start(), calls=%async_computation.2 | async-start | bytes 1114112 | tf_op jit(solution)/shard_map/reduce_scatter | solution.py:88
  208.1 6.0 %copy-start.6 = (bf16[2,256,2,4096]{3,1,0,2:T(8,128)(2,1)S(1)}, bf16[2,256,2,4096]{3,1,0,2:T(8,128)(2,1)}, u32[]{:S(2)}) copy-start(bf16[2,256,2,4096]{3,1,0,2:T(8,128)(2,1)} %all-gather.2.cloned.1.call-done) | copy-start | bytes 25165828
  211.2 4.3 %copy-start = (f32[9,2,8,1,4096]{4,0,2,1,3:T(8,128)}, f32[9,2,8,1,4096]{4,0,2,1,3:T(8,128)S(1)}, u32[]{:S(2)}) copy-start(f32[9,2,8,1,4096]{4,0,2,1,3:T(8,128)S(1)} %convolution_bitcast_fusion) | copy-start | bytes 7077892
  214.1 1.4 copy-start.5
  215.5 1.4 copy-start.4
Sparse Core Ops, SparseCore 0:
  17.8 190.2 all-gather.1
  219.9 80.1 reduce-scatter.1
where the time goes:
time: 309 us; the launch traced here: 308 us
  waiting for transfers between devices  245 us (79%)
  local copies, waits for them, and re-layouts  19.5 us (6%)
  between operations  14.5 us (5%)
  matrix products  13.3 us (4%)
  other arithmetic  11.4 us (4%)
  starting transfers between devices  4.44 us (1%)
    all_gather x1, waiting for transfers between devices, body(): signal = lax.all_gather(source, 'chan', axis=1, tiled=True)  185 us
    reduce_scatter x1, waiting for transfers between devices, body(): lax.psum_scatter(local_grad, 'slab', scatter_dimension=2, tiled=True)  60.7 us
    unnamed x35, local copies, waits for them, and re-layouts  11.8 us
    dot_general x3, matrix products, body(): jnp.einsum('tck,bkdp->tbcdp', weights[9 * depth_tap:9 * depth_tap + 9], b...  9.15 us
  transfers between devices with their start and end apart: 4, of which 2 were waited for; matrix products, arithmetic and copies ran while one was open for 10% of the time, Pallas kernels for 0%

commit v1 on v0

--- a/solution.py
+++ b/solution.py
@@ -5,6 +5,13 @@
 from jax.sharding import PartitionSpec as P
 
 EDGE = 128
+
+
+def all_by_exchange(x, axis, dim):
+    size = lax.axis_size(axis)
+    parts = jnp.stack([x for _ in range(size)])
+    parts = lax.all_to_all(parts, axis, split_axis=0, concat_axis=0)
+    return jnp.concatenate(parts, axis=dim)
 
 
 def from_behind(x, axis, by):
@@ -69,7 +76,7 @@
     depth_views = (odd_before, even_planes, odd_planes)
     following = from_behind(out_grad[:, :, 0], "slab", -1)
     source = jnp.concatenate([out_grad, following[:, :, None]], axis=2)
-    signal = lax.all_gather(source, "chan", axis=1, tiled=True)
+    signal = all_by_exchange(source, "chan", 1)
     own_planes = signal[:, :, :out_planes]
     pieces = []
     for depth_tap in range(3):

time: 309 us -> 326 us (1.055)
  local copies, waits for them, and re-layouts: 19.5 us -> 31.9 us
  starting transfers between devices: 4.44 us -> 13.6 us
    all_gather x1 -> x0, waiting for transfers between devices: 185 us -> none  [body(): signal = lax.all_gather(source, 'chan', axis=1, tiled=True)]
    all_to_all x0 -> x1, waiting for transfers between devices: none -> 180 us  [all_by_exchange(): parts = lax.all_to_all(parts, axis, split_axis=0, concat_axis=0)]
    all_to_all x0 -> x1, starting transfers between devices: none -> 8.99 us  [all_by_exchange(): parts = lax.all_to_all(parts, axis, split_axis=0, concat_axis=0)]
    reshape x0 -> x1, local copies, waits for them, and re-layouts: none -> 7.71 us  [all_by_exchange(): return jnp.concatenate(parts, axis=dim)]
    another operation x1 -> x2, local copies, waits for them, and re-layouts: 0.25 us -> 4.51 us  [the longest x1 4.26 us: all_by_exchange(): parts = jnp.stack([x for _ in range(size)])]
  transfers between devices with their start and end apart: 4 -> 4, of which waited for: 2 -> 2; matrix products, arithmetic and copies ran while one was open for 10% -> 11% of each run, Pallas kernels for 0% -> 0%
where the time goes in v1:
time: 326 us
  waiting for transfers between devices  242 us (74%)
  local copies, waits for them, and re-layouts  31.9 us (10%)
  between operations  14.5 us (4%)
  starting transfers between devices  13.6 us (4%)
  matrix products  13.4 us (4%)
  other arithmetic  10.7 us (3%)
    all_to_all x1, waiting for transfers between devices, all_by_exchange(): parts = lax.all_to_all(parts, axis, split_axis=0, concat_axis=0)  180 us
    reduce_scatter x1, waiting for transfers between devices, body(): lax.psum_scatter(local_grad, 'slab', scatter_dimension=2, tiled=True)  61.1 us
    unnamed x35, local copies, waits for them, and re-layouts  11.8 us
    dot_general x3, matrix products, body(): jnp.einsum('tck,bkdp->tbcdp', weights[9 * depth_tap:9 * depth_tap + 9], b...  9.18 us
    all_to_all x1, starting transfers between devices, all_by_exchange(): parts = lax.all_to_all(parts, axis, split_axis=0, concat_axis=0)  8.99 us
    reshape x1, local copies, waits for them, and re-layouts, all_by_exchange(): return jnp.concatenate(parts, axis=dim)  7.71 us
  transfers between devices with their start and end apart: 4, of which 2 were waited for; matrix products, arithmetic and copies ran while one was open for 11% of the time, Pallas kernels for 0%

profile of v1, /device:TPU:8, one launch (start us, length us, event | category | flops | bytes accessed | tf_op | source)
XLA Modules:
  0.0 325.7 jit_solution(4392997318855685547)
XLA Ops:
  7.2 1.3 collective-permute-start
  8.5 1.8 copy.116
  10.4 3.1 collective-permute-start.1
  14.3 0.8 bitcast_dynamic-update-slice_fusion.10
  15.1 0.9 bitcast_dynamic-update-slice_fusion.8
  16.0 0.8 bitcast_dynamic-update-slice_fusion.7
  16.9 4.3 %stack.118 = bf16[16,2,16,2,4096]{4,2,1,3,0:T(8,128)(2,1)} broadcast(bf16[2,16,2,4096]{3,1,0,2:T(8,128)(2,1)S(1)} %copy.33), dimensions={1,2,3,4} | broadcast | bytes 8912896 | tf_op jit(solution)/shard_map/stack | solution.py:12
  21.1 9.0 %all-to-all-start = ((bf16[16,2,16,2,4096]{4,2,1,3,0:T(8,128)(2,1)}), bf16[16,2,16,2,4096]{4,2,1,3,0:T(8,128)(2,1)}, u32[]{:S(2)}, u32[]{:S(2)}) async-start(bf16[16,2,16,2,4096]{4,2,1,3,0:T(8,128)(2,1)} %stack.118), calls=%async_computation | async-start | bytes 16777216 | tf_op jit(solution)/shard_map/all_to_all | solution.py:13
  30.4 0.8 bitcast_dynamic-update-slice_fusion.6
  31.1 0.7 fusion.56
  31.8 0.7 fusion.55
  32.4 0.8 bitcast_dynamic-update-slice_fusion.5
  33.2 0.6 fusion.54
  33.8 0.7 fusion.58
  34.5 0.7 fusion.53
  36.1 180.5 %all-to-all-done = bf16[16,2,16,2,4096]{4,2,1,3,0:T(8,128)(2,1)} async-done(((bf16[16,2,16,2,4096]{4,2,1,3,0:T(8,128)(2,1)}), bf16[16,2,16,2,4096]{4,2,1,3,0:T(8,128)(2,1)}, u32[]{:S(2)}, u32[]{:S(2)}) %all-to-all-start) | async-done | bytes 8388640 | tf_op jit(solution)/shard_map/all_to_all | solution.py:13
  216.5 7.7 %copy.34 = bf16[2,16,16,2,4096]{4,2,1,0,3:T(8,128)(2,1)} copy(bf16[2,16,16,2,4096]{4,2,0,3,1:T(8,128)(2,1)} %bitcast.2) | data formatting | bytes 16777216 | tf_op jit(solution)/shard_map/reshape | solution.py:14
  224.2 3.1 convolution_bitcast_fusion
  227.3 1.5 fusion.72
  229.1 1.1 copy-done
  230.8 1.4 fusion.26
  232.2 1.4 fusion.16
  233.6 1.4 fusion.21
  235.0 1.4 copy.60
  236.4 3.0 convolution_bitcast_fusion.2
  239.7 3.0 convolution_bitcast_fusion.1
  247.5 1.4 pad_add_fusion.2
  248.9 3.3 %fusion.52 = (bf16[2,8,1,4096]{3,2,1,0:T(2,128)(2,1)S(1)}, bf16[2,8,1,4096]{3,2,1,0:T(2,128)(2,1)S(1)}) fusion(f32[9,2,8,1,4096]{4,0,2,1,3:T(8,128)} %copy-done.1, f32[2,8,1,4032]{3,2,1,0:T(1,128)S(1)} %slice.342, f32[2,8,1,4095]{3,2,1,0:T(1,128)S(1)} %pad_add_fusion.2, pred[4096]{0:T(1024)(128)(4,1)S(1)} %fusion.70, f32[2,8,1,4032]{3,2,1,0:T(1,128)S(1)} %slice.345), kind=kLoop, calls=%fused_computation.84 | loop fusion | flops 393216 | bytes 1568704 | tf_op jit(solution)/shard_map/convert.5
  252.2 1.1 pad_maximum_fusion
  254.1 2.1 copy.61
  256.2 61.1 %reduce-scatter.2.cloned.1.call-done = f32[27,8,16]{0,1,2:T(8,128)} async-done(((f32[27,8,256]{0,1,2:T(8,128)}), f32[27,8,16]{0,1,2:T(8,128)}) %reduce-scatter.2.cloned.1.call-update) | async-done | bytes 13840 | tf_op jit(solution)/shard_map/reduce_scatter | solution.py:95
  317.3 0.8 broadcast_multiply_fusion
  (75 shorter events, 9.0 us)
Async XLA Ops:
  7.2 9.6 %collective-permute-start = (bf16[2,16,4096]{2,1,0:T(8,128)(2,1)}, bf16[2,16,4096]{2,1,0:T(8,128)(2,1)S(1)}, u32[]{:S(2)}, u32[]{:S(2)}) collective-permute-start(bf16[2,16,4096]{2,1,0:T(8,128)(2,1)} %bitcast.314), channel_id=1, source_target_pairs={{16,0},{32,16},{48,32},{64,48},{80,64},{96,80},{112,96},{128,112},... | collective-permute-start | bytes 786440 | tf_op jit(solution)/shard_map/ppermute | solution.py:20
  10.4 24.9 %collective-permute-start.1 = (bf16[2,8,16384]{2,1,0:T(8,128)(2,1)S(1)}, bf16[2,8,16384]{2,1,0:T(8,128)(2,1)S(1)}, u32[]{:S(2)}, u32[]{:S(2)}) collective-permute-start(bf16[2,8,16384]{2,1,0:T(8,128)(2,1)S(1)} %get-tuple-element.32), channel_id=1, source_target_pairs={{0,16},{16,32},{32,48},{48,64},{64,80},{80,96},{96,112},{112,128},... | collective-permute-start | bytes 1572872 | tf_op jit(solution)/shard_map/ppermute | solution.py:20
  13.9 2.8 copy-start.2
  15.1 1.7 copy-start.4
  21.1 195.4 %all-to-all-start = ((bf16[16,2,16,2,4096]{4,2,1,3,0:T(8,128)(2,1)}), bf16[16,2,16,2,4096]{4,2,1,3,0:T(8,128)(2,1)}, u32[]{:S(2)}, u32[]{:S(2)}) async-start(bf16[16,2,16,2,4096]{4,2,1,3,0:T(8,128)(2,1)} %stack.118), calls=%async_computation | async-start | bytes 16777216 | tf_op jit(solution)/shard_map/all_to_all | solution.py:13
  30.1 5.1 %copy-start.3 = (bf16[27,8,256]{2,1,0:T(8,128)(2,1)S(1)}, bf16[27,8,256]{2,1,0:T(8,128)(2,1)}, u32[]{:S(2)}) copy-start(bf16[27,8,256]{2,1,0:T(8,128)(2,1)} %param.5) | copy-start | bytes 331780
  30.1 287.2 %reduce-scatter.2.cloned.1.call-start = ((), (), s32[]{:S(2)}) async-start(), calls=%async_computation.2 | async-start | bytes 1114112 | tf_op jit(solution)/shard_map/reduce_scatter | solution.py:95
  224.2 6.0 %copy-start = (bf16[2,16,16,2,4096]{4,2,1,0,3:T(8,128)(2,1)S(1)}, bf16[2,16,16,2,4096]{4,2,1,0,3:T(8,128)(2,1)}, u32[]{:S(2)}) copy-start(bf16[2,16,16,2,4096]{4,2,1,0,3:T(8,128)(2,1)} %copy.34) | copy-start | bytes 25165828
  227.3 4.8 %copy-start.1 = (f32[9,2,8,1,4096]{4,0,2,1,3:T(8,128)}, f32[9,2,8,1,4096]{4,0,2,1,3:T(8,128)S(1)}, u32[]{:S(2)}) copy-start(f32[9,2,8,1,4096]{4,0,2,1,3:T(8,128)S(1)} %convolution_bitcast_fusion) | copy-start | bytes 7077892
  227.3 3.4 %copy-start.5 = (bf16[9,2,8,1,4096]{4,2,1,3,0:T(8,128)(2,1)S(1)}, bf16[9,2,8,1,4096]{4,2,1,3,0:T(8,128)(2,1)}, u32[]{:S(2)}) copy-start(bf16[9,2,8,1,4096]{4,2,1,3,0:T(8,128)(2,1)} %get-tuple-element.60) | copy-start | bytes 3538948
  230.8 1.4 copy-start.6
Sparse Core Ops, SparseCore 0:
  236.6 80.7 reduce-scatter.1
